TPU v7x, 32 devices: a whole 2x2x4 slice. The times are simulated.
32 devices in a mesh: dp: 2 (over x), fsdp: 16 (over z, y, core).
Axes of the slice: x: 2, y: 2, z: 4, core: 2. Of those that a mesh axis runs over, the one named last changes fastest.
Arguments:
- tokens: bfloat16 [18432, 768], P(('dp', 'fsdp')), may hold values from -6 to 6
- gain_attn: bfloat16 [768], P(('dp', 'fsdp')), may hold values from 0.25 to 1.75
- w_qkv: bfloat16 [768, 2304], P(('dp', 'fsdp')), may hold values from -0.21875 to 0.21875
- w_proj: bfloat16 [768, 768], P(('dp', 'fsdp')), may hold values from -2.5 to 2.5
- gain_moe: bfloat16 [768], P(('dp', 'fsdp')), may hold values from 0.25 to 1.75
- w_router: bfloat16 [768, 8], P(('dp', 'fsdp')), may hold values from -0.15625 to 0.15625
- w_in: bfloat16 [8, 768, 3072], P('dp', 'fsdp'), may hold values from -0.21875 to 0.21875
- w_out: bfloat16 [8, 3072, 768], P('dp', 'fsdp'), may hold values from -0.875 to 0.875
- routes: int32 [18432, 2], P(('dp', 'fsdp')), may hold values from 0 to 7, as said below
- slot_ids: int32 [18432, 2], P(('dp', 'fsdp')), may hold values from 0 to 152, as said below
- cotangent: bfloat16 [18432, 768], P(('dp', 'fsdp')), may hold values from -6 to 6
Outputs:
- output: bfloat16 [18432, 768], P(('dp', 'fsdp'))
- grad_tokens: float32 [18432, 768], P(('dp', 'fsdp'))
- d_gain_attn: float32 [768], P(('dp', 'fsdp'))
- d_qkv: float32 [768, 2304], P(('dp', 'fsdp'))
- d_proj: float32 [768, 768], P(('dp', 'fsdp'))
- d_gain_moe: float32 [768], P(('dp', 'fsdp'))
- d_router: float32 [768, 8], P(('dp', 'fsdp'))
- d_in: float32 [8, 768, 3072], P('dp', 'fsdp')
- d_out: float32 [8, 3072, 768], P('dp', 'fsdp')
Inputs may be any that keep to these rules, and one draw needn't show every extreme that they name: `routes`: each row names two different experts. `slot_ids`: among the 576 patches of one device, the pairs routed to one expert hold the distinct slots 0, 1, 2, ... in some priority order; a pair beyond the 152 slots holds 152 and is dropped. On every device some expert gets more than 152 pairs.
All inputs are finite; a program needn't handle non-finite values.
Results may differ from a plain program's by a relative error of at most 0.017.
Values may be sent and summed in bfloat16 or wider, within the bound.
No kernel may reach another device: no remote copies, remote signals or barrier semaphores. Data moves between devices by JAX's collectives and lax.ppermute only.
A program may use at most 320 MiB of HBM per device.

v0:
```python
import jax
import jax.numpy as jnp
from jax import lax
from jax.sharding import PartitionSpec as P

HEADS = 12
HEAD_DIM = 64
EXPERTS = 8
SEQ = 576
CAP = 152
norm_epsilon = 1e-06


def norm_parts(values):
    centre = values - jnp.mean(values, axis=-1, keepdims=True)
    inverse = lax.rsqrt(jnp.mean(centre * centre, axis=-1, keepdims=True) + norm_epsilon)
    return (centre * inverse, inverse)


def norm_back(grad_normed, normed, inverse):
    mean_grad = jnp.mean(grad_normed, axis=-1, keepdims=True)
    mean_cross = jnp.mean(grad_normed * normed, axis=-1, keepdims=True)
    return (grad_normed - mean_grad - normed * mean_cross) * inverse


def gelu_tanh(values):
    return jax.nn.gelu(values, approximate=True)


def head_forward(operands):
    queries, keys_head, values_head = operands
    scores = jnp.einsum(
        "isd,itd->ist", queries, keys_head, preferred_element_type=jnp.float32
    ) * HEAD_DIM ** (-0.5)
    largest = jnp.max(scores, axis=-1, keepdims=True)
    powers = jnp.exp(scores - largest)
    totals = jnp.sum(powers, axis=-1, keepdims=True)
    attn_probs = (powers / totals).astype(jnp.bfloat16)
    head_out = jnp.einsum(
        "ist,itd->isd", attn_probs, values_head, preferred_element_type=jnp.float32
    )
    return (head_out.astype(jnp.bfloat16), (largest + jnp.log(totals))[..., 0])


def head_backward(operands):
    queries, keys_head, values_head, grad_head, log_total = operands
    scores = jnp.einsum(
        "isd,itd->ist", queries, keys_head, preferred_element_type=jnp.float32
    ) * HEAD_DIM ** (-0.5)
    attn_probs = jnp.exp(scores - log_total[..., None])
    grad_probs = jnp.einsum(
        "isd,itd->ist", grad_head, values_head, preferred_element_type=jnp.float32
    )
    row_terms = jnp.sum(attn_probs * grad_probs, axis=-1, keepdims=True)
    grad_scores = (attn_probs * (grad_probs - row_terms)).astype(jnp.bfloat16)
    grad_query = jnp.einsum(
        "ist,itd->isd", grad_scores, keys_head, preferred_element_type=jnp.float32
    ) * HEAD_DIM ** (-0.5)
    grad_key = jnp.einsum(
        "ist,isd->itd", grad_scores, queries, preferred_element_type=jnp.float32
    ) * HEAD_DIM ** (-0.5)
    grad_value = jnp.einsum(
        "ist,isd->itd",
        attn_probs.astype(jnp.bfloat16),
        grad_head,
        preferred_element_type=jnp.float32,
    )
    return (grad_query, grad_key, grad_value)


def expert_forward(expert_rows, w_up, w_down):
    pre_act = jnp.einsum("ecd,edf->ecf", expert_rows, w_up, preferred_element_type=jnp.float32)
    hidden = gelu_tanh(pre_act).astype(jnp.bfloat16)
    result = jnp.einsum("ecf,efd->ecd", hidden, w_down, preferred_element_type=jnp.float32).astype(
        jnp.bfloat16
    )
    return (pre_act, hidden, result)


def expert_backward(expert_rows, pre_act, hidden, grad_result, w_up, w_down):
    grad_hidden = jnp.einsum(
        "ecd,efd->ecf", grad_result, w_down, preferred_element_type=jnp.float32
    )
    ignored, pull_back = jax.vjp(gelu_tanh, pre_act)
    grad_pre = pull_back(grad_hidden)[0].astype(jnp.bfloat16)
    grad_down = jnp.einsum("ecf,ecd->efd", hidden, grad_result, preferred_element_type=jnp.float32)
    grad_up = jnp.einsum("ecd,ecf->edf", expert_rows, grad_pre, preferred_element_type=jnp.float32)
    grad_rows = jnp.einsum(
        "ecf,edf->ecd", grad_pre, w_up, preferred_element_type=jnp.float32
    ).astype(jnp.bfloat16)
    return (grad_up, grad_down, grad_rows)


def gather_dense(gain_attn, w_qkv, w_proj, gain_moe, w_router):
    return (
        lax.all_gather(gain_attn, ("dp", "fsdp"), axis=0, tiled=True),
        lax.all_gather(w_qkv, ("dp", "fsdp"), axis=0, tiled=True),
        lax.all_gather(w_proj, ("dp", "fsdp"), axis=0, tiled=True),
        lax.all_gather(gain_moe, ("dp", "fsdp"), axis=0, tiled=True),
        lax.all_gather(w_router, ("dp", "fsdp"), axis=0, tiled=True),
    )


def gather_experts(w_in, w_out):
    local_pair = (w_in, w_out)
    return (
        lax.all_gather(local_pair[0], "fsdp", axis=1, tiled=True),
        lax.all_gather(local_pair[1], "fsdp", axis=1, tiled=True),
    )


def reduce_experts(grad_up, grad_down):
    reduced = (
        lax.psum_scatter(
            grad_up.astype(jnp.bfloat16), "fsdp", scatter_dimension=1, tiled=True
        ).astype(jnp.float32),
        lax.psum_scatter(
            grad_down.astype(jnp.bfloat16), "fsdp", scatter_dimension=1, tiled=True
        ).astype(jnp.float32),
    )
    return reduced


def per_device(
    tokens, gain_attn, w_qkv, w_proj, gain_moe, w_router, w_in, w_out, routes, slot_ids, cotangent
):
    dense_full = gather_dense(gain_attn, w_qkv, w_proj, gain_moe, w_router)
    expert_weights = gather_experts(w_in, w_out)
    rows_here = tokens.shape[0]
    images = rows_here // SEQ
    residual = tokens.astype(jnp.float32)
    normed_one, inverse_one = norm_parts(residual)
    gain_one = dense_full[0].astype(jnp.float32)
    act_one = (normed_one * gain_one).astype(jnp.bfloat16)
    qkv = jnp.dot(act_one, dense_full[1], preferred_element_type=jnp.float32).astype(jnp.bfloat16)
    split_qkv = qkv.reshape(images, SEQ, 3, HEADS, HEAD_DIM).transpose(2, 3, 0, 1, 4)
    head_out, head_lse = lax.map(head_forward, (split_qkv[0], split_qkv[1], split_qkv[2]))
    attended = head_out.transpose(1, 2, 0, 3).reshape(rows_here, -1)
    resid_mid = residual + jnp.dot(attended, dense_full[2], preferred_element_type=jnp.float32)
    normed_two, inverse_two = norm_parts(resid_mid)
    gain_two = dense_full[3].astype(jnp.float32)
    act_two = (normed_two * gain_two).astype(jnp.bfloat16)
    logits = jnp.dot(act_two, dense_full[4], preferred_element_type=jnp.float32)
    router = jax.nn.softmax(logits, axis=-1)
    expert_ids = lax.broadcasted_iota(jnp.int32, (1, 1, EXPERTS), 2)
    chosen = routes[:, :, None] == expert_ids
    gate_values = jnp.sum(jnp.where(chosen, router[:, None, :], 0.0), axis=-1)
    gates_low = gate_values.astype(jnp.bfloat16)
    slot_count = EXPERTS * CAP
    columns = lax.broadcasted_iota(jnp.int32, (1, 1, slot_count), 2)
    live_pair = slot_ids < CAP
    targets = routes * CAP + slot_ids
    matches = (targets[:, :, None] == columns) & live_pair[:, :, None]
    dispatch = jnp.sum(matches.astype(jnp.bfloat16), axis=1)
    combine = jnp.sum(
        jnp.where(matches, gates_low[:, :, None], jnp.zeros((), jnp.bfloat16)), axis=1
    )
    slot_rows = (
        jnp.einsum("tx,td->xd", dispatch, act_two, preferred_element_type=jnp.float32)
        .astype(jnp.bfloat16)
        .reshape(EXPERTS, CAP, -1)
    )
    expert_rows = lax.all_to_all(slot_rows, "dp", split_axis=0, concat_axis=1, tiled=True)
    pre_act, hidden, result = expert_forward(expert_rows, expert_weights[0], expert_weights[1])
    slot_result = lax.all_to_all(result, "dp", split_axis=1, concat_axis=0, tiled=True)
    flat_result = slot_result.reshape(slot_count, -1)
    moe_sum = jnp.einsum("tx,xd->td", combine, flat_result, preferred_element_type=jnp.float32)
    output = (resid_mid + moe_sum).astype(jnp.bfloat16)
    dense_full = gather_dense(gain_attn, w_qkv, w_proj, gain_moe, w_router)
    expert_weights = gather_experts(w_in, w_out)
    grad_slots = (
        jnp.einsum("tx,td->xd", combine, cotangent, preferred_element_type=jnp.float32)
        .astype(jnp.bfloat16)
        .reshape(EXPERTS, CAP, -1)
    )
    picked = flat_result[jnp.clip(targets, 0, slot_count - 1)]
    grad_gates = jnp.where(
        live_pair,
        jnp.einsum("tkd,td->tk", picked, cotangent, preferred_element_type=jnp.float32),
        0.0,
    )
    grad_router = jnp.sum(jnp.where(chosen, grad_gates[:, :, None], 0.0), axis=1)
    grad_logits = (
        router * (grad_router - jnp.sum(router * grad_router, axis=-1, keepdims=True))
    ).astype(jnp.bfloat16)
    d_router = jnp.einsum("td,te->de", act_two, grad_logits, preferred_element_type=jnp.float32)
    grad_act_two = jnp.einsum(
        "te,de->td", grad_logits, dense_full[4], preferred_element_type=jnp.float32
    )
    grad_expert = lax.all_to_all(grad_slots, "dp", split_axis=0, concat_axis=1, tiled=True)
    grad_up, grad_down, grad_rows = expert_backward(
        expert_rows, pre_act, hidden, grad_expert, expert_weights[0], expert_weights[1]
    )
    grad_rows = lax.all_to_all(grad_rows, "dp", split_axis=1, concat_axis=0, tiled=True)
    grad_act_two = grad_act_two + jnp.einsum(
        "tx,xd->td", dispatch, grad_rows.reshape(slot_count, -1), preferred_element_type=jnp.float32
    )
    d_gain_moe = jnp.sum(grad_act_two * normed_two, axis=0)
    grad_mid = cotangent.astype(jnp.float32) + norm_back(
        grad_act_two * gain_two, normed_two, inverse_two
    )
    grad_mid_low = grad_mid.astype(jnp.bfloat16)
    d_proj = jnp.einsum("td,te->de", attended, grad_mid_low, preferred_element_type=jnp.float32)
    grad_attended = jnp.einsum(
        "te,de->td", grad_mid_low, dense_full[2], preferred_element_type=jnp.float32
    ).astype(jnp.bfloat16)
    grad_heads = grad_attended.reshape(images, SEQ, HEADS, HEAD_DIM).transpose(2, 0, 1, 3)
    grad_query, grad_key, grad_value = lax.map(
        head_backward, (split_qkv[0], split_qkv[1], split_qkv[2], grad_heads, head_lse)
    )
    grad_qkv = (
        jnp.stack([grad_query, grad_key, grad_value])
        .transpose(2, 3, 0, 1, 4)
        .reshape(rows_here, -1)
        .astype(jnp.bfloat16)
    )
    d_qkv = jnp.einsum("td,te->de", act_one, grad_qkv, preferred_element_type=jnp.float32)
    grad_act_one = jnp.einsum(
        "te,de->td", grad_qkv, dense_full[1], preferred_element_type=jnp.float32
    )
    d_gain_attn = jnp.sum(grad_act_one * normed_one, axis=0)
    grad_tokens = grad_mid + norm_back(grad_act_one * gain_one, normed_one, inverse_one)
    dense_grads = (
        lax.psum_scatter(d_gain_attn, ("dp", "fsdp"), scatter_dimension=0, tiled=True),
        lax.psum_scatter(d_qkv, ("dp", "fsdp"), scatter_dimension=0, tiled=True),
        lax.psum_scatter(d_proj, ("dp", "fsdp"), scatter_dimension=0, tiled=True),
        lax.psum_scatter(d_gain_moe, ("dp", "fsdp"), scatter_dimension=0, tiled=True),
        lax.psum_scatter(d_router, ("dp", "fsdp"), scatter_dimension=0, tiled=True),
    )
    expert_grads = reduce_experts(grad_up, grad_down)
    return (
        output,
        grad_tokens,
        dense_grads[0],
        dense_grads[1],
        dense_grads[2],
        dense_grads[3],
        dense_grads[4],
        expert_grads[0],
        expert_grads[1],
    )


def solution(mesh):
    in_specs = (
        P(("dp", "fsdp"), None),
        P(("dp", "fsdp")),
        P(("dp", "fsdp"), None),
        P(("dp", "fsdp"), None),
        P(("dp", "fsdp")),
        P(("dp", "fsdp"), None),
        P("dp", "fsdp", None),
        P("dp", "fsdp", None),
        P(("dp", "fsdp"), None),
        P(("dp", "fsdp"), None),
        P(("dp", "fsdp"), None),
    )
    out_specs = (
        P(("dp", "fsdp"), None),
        P(("dp", "fsdp"), None),
        P(("dp", "fsdp")),
        P(("dp", "fsdp"), None),
        P(("dp", "fsdp"), None),
        P(("dp", "fsdp")),
        P(("dp", "fsdp"), None),
        P("dp", "fsdp", None),
        P("dp", "fsdp", None),
    )
    return jax.shard_map(
        per_device, mesh=mesh, in_specs=in_specs, out_specs=out_specs, check_vma=False
    )
```

profile of v0, /device:TPU:0, one launch (start us, length us, event | category | flops | bytes accessed | tf_op | source)
XLA Modules:
  0.0 1001.7 jit_solution(7998535637937780949)
XLA Ops:
  10.6 42.0 %all-reduce.6 = (bf16[768]{0:T(1024)(128)(2,1)S(1)}, bf16[768]{0:T(1024)(128)(2,1)S(1)}) all-reduce(bf16[768]{0:T(1024)(128)(2,1)S(1)} %dynamic-update-slice, bf16[768]{0:T(1024)(128)(2,1)S(1)} %dynamic-update-slice.1), channel_id=1, replica_groups=mesh['dp'=2,'fsdp'=16] {'dp','fsdp'}, use_global_device_ids=true, to_apply=%add | all-reduce | flops 1536 | bytes 6144
  52.6 40.8 %all-gather = bf16[32,24,8]{1,2,0:T(8,128)(2,1)S(1)} all-gather(bf16[1,24,8]{1,2,0:T(8,128)(2,1)S(1)} %bitcast.199), channel_id=1, replica_groups=mesh['dp'=2,'fsdp'=16] {'dp','fsdp'}, dimensions={0}, use_global_device_ids=true | all-gather | bytes 12672 | tf_op jit(solution)/shard_map/all_gather | solution.py:100
  95.4 5.9 convolution_convert_fusion.3
  113.4 37.9 %while.26 = (s32[]{:T(128)}, bf16[12,1,576,64]{2,3,1,0:T(8,128)(2,1)}, f32[12,1,576]{2,1,0:T(1,128)}, bf16[12,1,576,64]{3,2,1,0:T(8,128)(2,1)S(1)}, bf16[12,1,57...) while((s32[]{:T(128)}, bf16[12,1,576,64]{2,3,1,0:T(8,128)(2,1)}, ...), condition=%wide.region_5.6_spmd, body=%wide.region_2.5_spmd.sunk | while | flops 87293376 | bytes 4531033 | solution.py:137
  171.9 18.5 %all-to-all-done.2 = bf16[8,152,768]{2,1,0:T(8,128)(2,1)S(1)} async-done(((bf16[8,152,768]{2,1,0:T(8,128)(2,1)}), bf16[8,152,768]{2,1,0:T(8,128)(2,1)S(1)}, u32[]{:S(2)}, u32[]{:S(2)}) %all-to-all-start.2) | async-done | bytes 1867808 | tf_op jit(solution)/shard_map/all_to_all | solution.py:190
  198.6 20.2 %all-to-all-done = bf16[8,152,768]{2,1,0:T(8,128)(2,1)} async-done(((bf16[8,152,768]{2,1,0:T(8,128)(2,1)}), bf16[8,152,768]{2,1,0:T(8,128)(2,1)}, u32[]{:S(2)}, u32[]{:S(2)}) %all-to-all-start) | async-done | bytes 1867808 | tf_op jit(solution)/shard_map/all_to_all | solution.py:163
  221.7 7.1 all-gather.12.cloned.1.call-done
  228.8 12.9 %fusion.77 = f32[4,304,3072]{2,1,0:T(8,128)} fusion(bf16[4,304,768]{2,1,0:T(8,128)(2,1)S(1)} %bitcast.182, bf16[4,3072,768]{2,1,0:T(8,128)(2,1)} %all-gather.12.cloned.1.call-done), kind=kOutput, calls=%fused_computation.141 | convolution fusion | flops 5737807872 | bytes 35684352 | tf_op jit(solution)/shard_map/ecd,efd->ecf/dot_general | solution.py:81
  241.7 87.4 %all-gather.10.cloned.1.call-done = bf16[4,768,3072]{2,1,0:T(8,128)(2,1)} async-done(((bf16[4,48,3072]{2,1,0:T(8,128)(2,1)}), bf16[4,768,3072]{2,1,0:T(8,128)(2,1)}) %all-gather.10.cloned.1.call-update) | async-done | bytes 18874384 | tf_op jit(solution)/shard_map/all_gather | solution.py:107
  329.1 26.9 %fusion.43 = (bf16[4,304,3072]{2,1,0:T(8,128)(2,1)}, f32[4,304,3072]{2,1,0:T(8,128)}) fusion(f32[4,304,3072]{2,1,0:T(8,128)} %fusion.77, bf16[4,304,768]{2,1,0:T(8,128)(2,1)} %bitcast.192, bf16[4,768,3072]{2,1,0:T(8,128)(2,1)} %all-gather.10.cloned.1.call-done), kind=kOutput, calls=%fused_computation.59 | convolution fusion | flops 5812518912 | bytes 58097664 | tf_op jit(solution)/shard_map/ecd,edf->ecf/dot_general | solution.py:72
  356.0 16.5 %convolution_convert_fusion.2 = bf16[4,768,3072]{2,1,0:T(8,128)(2,1)} fusion(bf16[4,304,768]{2,1,0:T(8,128)(2,1)} %bitcast.193, bf16[4,304,3072]{2,1,0:T(8,128)(2,1)} %get-tuple-element.212), kind=kOutput, calls=%fused_computation.62 | convolution fusion | flops 5747245056 | bytes 28213248 | tf_op jit(solution)/shard_map/ecd,ecf->edf/dot_general | solution.py:87
  372.8 20.0 %convolution_convert_fusion.1 = bf16[4,3072,768]{2,1,0:T(8,128)(2,1)} fusion(bf16[4,304,768]{2,1,0:T(8,128)(2,1)S(1)} %bitcast.183, f32[4,304,3072]{2,1,0:T(8,128)} %get-tuple-element.213), kind=kOutput, calls=%fused_computation.61 | convolution fusion | flops 5780865024 | bytes 35684352 | tf_op jit(solution)/shard_map/ecf,ecd->efd/dot_general | solution.py:86
  392.9 19.3 %convolution_convert_fusion.7 = bf16[4,304,768]{2,1,0:T(8,128)(2,1)S(1)} fusion(bf16[4,3072,768]{2,1,0:T(8,128)(2,1)} %all-gather.12.cloned.1.call-done, f32[4,304,3072]{2,1,0:T(8,128)} %get-tuple-element.213), kind=kOutput, calls=%fused_computation.85 | convolution fusion | flops 5772361728 | bytes 35684352 | tf_op jit(solution)/shard_map/ecf,efd->ecd/dot_general | solution.py:74
  418.4 13.2 %convolution_convert_fusion.6 = bf16[4,304,768]{2,1,0:T(8,128)(2,1)} fusion(bf16[4,304,3072]{2,1,0:T(8,128)(2,1)} %get-tuple-element.212, bf16[4,768,3072]{2,1,0:T(8,128)(2,1)} %all-gather.10.cloned.1.call-done), kind=kOutput, calls=%fused_computation.84 | convolution fusion | flops 5738741760 | bytes 28213248 | tf_op jit(solution)/shard_map/ecf,edf->ecd/dot_general | solution.py:88
  435.3 6.1 all-to-all-done.1
  449.7 20.1 %all-to-all-done.3 = bf16[4,304,768]{2,0,1:T(4,128)(2,1)} async-done(((bf16[4,304,768]{2,0,1:T(4,128)(2,1)}), bf16[4,304,768]{2,0,1:T(4,128)(2,1)}, u32[]{:S(2)}, u32[]{:S(2)}) %all-to-all-start.3) | async-done | bytes 1867808 | tf_op jit(solution)/shard_map/all_to_all | solution.py:194
  482.4 6.0 fusion.62
  503.7 100.7 %while.27 = (s32[]{:T(128)}, bf16[12,1,576,64]{2,3,1,0:T(8,128)(2,1)}, bf16[12,1,576,64]{2,3,1,0:T(8,128)(2,1)}, bf16[12,1,576,64]{2,3,1,0:T(8,128)(2,1)}, bf16[...) while((s32[]{:T(128)}, ...), condition=%wide.region_19.20_spmd, body=%wide.region_17.19_spmd.sunk | while | flops 215064000 | bytes 11510129 | solution.py:208
  608.4 5.5 fusion.71
  615.2 7.2 fusion.60
  622.4 43.2 %all-reduce.5 = (f32[768]{0:T(1024)S(1)}, f32[768]{0:T(1024)S(1)}, f32[768,8]{0,1:T(8,128)S(1)}) all-reduce(f32[768]{0:T(1024)S(1)} %get-tuple-element.158, f32[768]{0:T(1024)S(1)} %get-tuple-element.156, f32[768,8]{0,1:T(8,128)S(1)} %fusion.79), channel_id=2, replica_groups=mesh['dp'=2,'fsdp'=16] {'dp','fsdp'}, use_global_device_ids=true, to_apply=%region_23.24.clone | all-reduce | flops 7680 | bytes 61440
  676.7 88.2 %reduce-scatter.12.cloned.1.call-done = bf16[4,192,768]{2,1,0:T(8,128)(2,1)} async-done(((bf16[4,3072,768]{2,1,0:T(8,128)(2,1)}), bf16[4,192,768]{2,1,0:T(8,128)(2,1)}) %reduce-scatter.12.cloned.1.call-update) | async-done | bytes 1179664 | tf_op jit(solution)/shard_map/reduce_scatter | solution.py:117
  767.8 101.8 %reduce-scatter.8.cloned.1.call-done = f32[24,768]{1,0:T(8,128)} async-done(((f32[768,768]{1,0:T(8,128)}), f32[24,768]{1,0:T(8,128)}) %reduce-scatter.8.cloned.1.call-update) | async-done | bytes 73744 | tf_op jit(solution)/shard_map/reduce_scatter | solution.py:226
  869.6 124.8 %reduce-scatter.6.cloned.1.call-done = f32[24,2304]{1,0:T(8,128)} async-done(((f32[768,2304]{1,0:T(8,128)}), f32[24,2304]{1,0:T(8,128)}) %reduce-scatter.6.cloned.1.call-update) | async-done | bytes 221200 | tf_op jit(solution)/shard_map/reduce_scatter | solution.py:225
  (316 shorter events, 252.4 us)
Async XLA Ops:
  7.2 45.4 %copy-start.34 = (bf16[24,8]{0,1:T(8,128)(2,1)S(1)}, bf16[24,8]{0,1:T(8,128)(2,1)}, u32[]{:S(2)}) copy-start(bf16[24,8]{0,1:T(8,128)(2,1)} %param.20) | copy-start | bytes 1156
  7.2 86.3 %copy-start.8 = (bf16[576,768]{1,0:T(8,128)(2,1)S(1)}, bf16[576,768]{1,0:T(8,128)(2,1)}, u32[]{:S(2)}) copy-start(bf16[576,768]{1,0:T(8,128)(2,1)} %param.15) | copy-start | bytes 2654212
  7.2 88.2 %all-gather.6.cloned.1.call-start = ((), (), s32[]{:S(2)}) async-start(), calls=%async_computation.8 | async-start | bytes 3649536 | tf_op jit(solution)/shard_map/all_gather | solution.py:97
  8.0 143.4 %all-gather.8.cloned.1.call-start = ((), (), s32[]{:S(2)}) async-start(), calls=%async_computation.9 | async-start | bytes 1216512 | tf_op jit(solution)/shard_map/all_gather | solution.py:98
  8.7 220.1 %all-gather.12.cloned.1.call-start = ((), (), s32[]{:S(2)}) async-start(), calls=%async_computation.11 | async-start | bytes 20054016 | tf_op jit(solution)/shard_map/all_gather | solution.py:108
  9.4 84.7 %copy-start.21 = (s32[576,2]{0,1:T(2,128)S(1)}, s32[576,2]{0,1:T(2,128)}, u32[]{:S(2)}) copy-start(s32[576,2]{0,1:T(2,128)} %param.24) | copy-start | bytes 13828
  9.4 85.3 %copy-start.23 = (s32[576,2]{0,1:T(2,128)S(1)}, s32[576,2]{0,1:T(2,128)}, u32[]{:S(2)}) copy-start(s32[576,2]{0,1:T(2,128)} %param.23) | copy-start | bytes 13828
  9.5 319.6 %all-gather.10.cloned.1.call-start = ((), (), s32[]{:S(2)}) async-start(), calls=%async_computation.10 | async-start | bytes 20054016 | tf_op jit(solution)/shard_map/all_gather | solution.py:107
  52.6 42.8 %copy-start.29 = (f32[768]{0:T(1024)}, f32[768]{0:T(1024)S(1)}, u32[]{:S(2)}) copy-start(f32[768]{0:T(1024)S(1)} %convert_element_type.101) | copy-start | bytes 9220
  151.3 4.2 copy-start.5
  156.7 10.9 %copy-start.6 = (bf16[576,768]{1,0:T(8,128)(2,1)}, bf16[576,768]{1,0:T(8,128)(2,1)S(1)}, u32[]{:S(2)}) copy-start(bf16[576,768]{1,0:T(8,128)(2,1)S(1)} %multiply_convert_fusion.2) | copy-start | bytes 2654212
  156.7 4.2 copy-start.19
  163.8 26.7 %all-to-all-start.2 = ((bf16[8,152,768]{2,1,0:T(8,128)(2,1)}), bf16[8,152,768]{2,1,0:T(8,128)(2,1)S(1)}, u32[]{:S(2)}, u32[]{:S(2)}) async-start(bf16[8,152,768]{2,1,0:T(8,128)(2,1)} %bitcast.194), calls=%async_computation.2 | async-start | bytes 3735552 | tf_op jit(solution)/shard_map/all_to_all | solution.py:190
  191.7 27.1 %all-to-all-start = ((bf16[8,152,768]{2,1,0:T(8,128)(2,1)}), bf16[8,152,768]{2,1,0:T(8,128)(2,1)}, u32[]{:S(2)}, u32[]{:S(2)}) async-start(bf16[8,152,768]{2,1,0:T(8,128)(2,1)} %bitcast.191), calls=%async_computation | async-start | bytes 3735552 | tf_op jit(solution)/shard_map/all_to_all | solution.py:163
  196.5 477.2 %reduce-scatter.10.cloned.1.call-start = ((), (), s32[]{:S(2)}) async-start(), calls=%async_computation.14 | async-start | bytes 20054016 | tf_op jit(solution)/shard_map/reduce_scatter | solution.py:114
  372.6 392.4 %reduce-scatter.12.cloned.1.call-start = ((), (), s32[]{:S(2)}) async-start(), calls=%async_computation.15 | async-start | bytes 20054016 | tf_op jit(solution)/shard_map/reduce_scatter | solution.py:117
  414.4 27.0 %all-to-all-start.1 = ((bf16[4,304,768]{2,0,1:T(4,128)(2,1)}), bf16[4,304,768]{2,0,1:T(4,128)(2,1)S(1)}, u32[]{:S(2)}, u32[]{:S(2)}) async-start(bf16[4,304,768]{2,0,1:T(4,128)(2,1)} %copy.108), calls=%async_computation.1 | async-start | bytes 3735552 | tf_op jit(solution)/shard_map/all_to_all | solution.py:165
  435.3 12.2 %copy-start.28 = (s32[576,2]{0,1:T(2,128)S(1)}, s32[576,2]{0,1:T(2,128)}, u32[]{:S(2)}) copy-start(s32[576,2]{0,1:T(2,128)} %get-tuple-element.199) | copy-start | bytes 13828
  442.6 27.1 %all-to-all-start.3 = ((bf16[4,304,768]{2,0,1:T(4,128)(2,1)}), bf16[4,304,768]{2,0,1:T(4,128)(2,1)}, u32[]{:S(2)}, u32[]{:S(2)}) async-start(bf16[4,304,768]{2,0,1:T(4,128)(2,1)} %copy.112), calls=%async_computation.3 | async-start | bytes 3735552 | tf_op jit(solution)/shard_map/all_to_all | solution.py:194
  447.4 422.2 %reduce-scatter.8.cloned.1.call-start = ((), (), s32[]{:S(2)}) async-start(), calls=%async_computation.13 | async-start | bytes 2433024 | tf_op jit(solution)/shard_map/reduce_scatter | solution.py:226
  482.4 7.1 copy-start.22
  482.4 7.3 copy-start.16
  503.4 491.0 %reduce-scatter.6.cloned.1.call-start = ((), (), s32[]{:S(2)}) async-start(), calls=%async_computation.12 | async-start | bytes 7299072 | tf_op jit(solution)/shard_map/reduce_scatter | solution.py:225
  615.2 52.2 %copy-start.10 = (bf16[576,768]{1,0:T(8,128)(2,1)S(1)}, bf16[576,768]{1,0:T(8,128)(2,1)}, u32[]{:S(2)}) copy-start(bf16[576,768]{1,0:T(8,128)(2,1)} %param.15) | copy-start | bytes 2654212
  (26 other events, 53.1 us)
Sparse Core Ops, SparseCore 0:
  10.9 62.6 all-gather.5
  76.6 52.6 all-gather.7
  130.9 97.8 all-gather.11
  230.2 98.8 all-gather.9
  372.7 194.0 reduce-scatter.9
  570.7 194.1 reduce-scatter.11
  770.8 98.7 reduce-scatter.7
  875.8 118.5 reduce-scatter.5
where the time goes:
time: 1010 us; the launch traced here: 1000 us
  waiting for transfers between devices  477 us (47%)
  matrix products  276 us (27%)
  blocking collectives  126 us (12%)
  local copies, waits for them, and re-layouts  66.9 us (7%)
  other arithmetic  22.4 us (2%)
  starting transfers between devices  18.3 us (2%)
  between operations  15.1 us (1%)
    reduce_scatter x1, waiting for transfers between devices, per_device(): lax.psum_scatter(d_qkv, ('dp', 'fsdp'), scatter_dimension=0, tiled=True)  125 us
    reduce_scatter x1, waiting for transfers between devices, per_device(): lax.psum_scatter(d_proj, ('dp', 'fsdp'), scatter_dimension=0, tiled=True)  102 us
    reduce_scatter x1, waiting for transfers between devices, reduce_experts(): lax.psum_scatter(grad_down.astype(jnp.bfloat16), 'fsdp', scatter_dimensio...  88.2 us
    all_gather x1, waiting for transfers between devices, gather_experts(): lax.all_gather(local_pair[0], 'fsdp', axis=1, tiled=True)  87.4 us
    unnamed x2, blocking collectives  85.2 us
    all_gather x1, blocking collectives, gather_dense(): lax.all_gather(w_router, ('dp', 'fsdp'), axis=0, tiled=True)  40.8 us
    dot_general x1, matrix products, expert_forward(): jnp.einsum('ecd,edf->ecf', expert_rows, w_up, preferred_element_type=jnp....  26.9 us
    dot_general x12, matrix products, head_forward(): jnp.einsum('ist,itd->isd', attn_probs, values_head, preferred_element_typ...  23.4 us
  transfers between devices with their start and end apart: 12, of which 9 were waited for; matrix products, arithmetic and copies ran while one was open for 31% of the time, Pallas kernels for 0%

commit v1 on v0

--- a/solution.py
+++ b/solution.py
@@ -9,6 +9,18 @@
 SEQ = 576
 CAP = 152
 norm_epsilon = 1e-06
+
+
+def collect(array, axis, dim):
+    ways, here = (lax.axis_size(axis), lax.axis_index(axis))
+    grown, reach = (array, 1)
+    while reach < ways:
+        theirs = lax.ppermute(grown, axis, [(d, d ^ reach) for d in range(ways)])
+        mine_first = jnp.concatenate([grown, theirs], axis=dim)
+        theirs_first = jnp.concatenate([theirs, grown], axis=dim)
+        grown = jnp.where(here & reach == 0, mine_first, theirs_first)
+        reach = 2 * reach
+    return grown
 
 
 def norm_parts(values):
@@ -104,7 +116,7 @@
 def gather_experts(w_in, w_out):
     local_pair = (w_in, w_out)
     return (
-        lax.all_gather(local_pair[0], "fsdp", axis=1, tiled=True),
+        collect(local_pair[0], "fsdp", 1),
         lax.all_gather(local_pair[1], "fsdp", axis=1, tiled=True),
     )
 

time: 1010 us -> 1430 us (1.42)
  waiting for transfers between devices: 477 us -> 725 us
  blocking collectives: 126 us -> 265 us
  other arithmetic: 22.4 us -> 43.9 us
    ppermute x0 -> x4, waiting for transfers between devices: none -> 347 us  [collect(): theirs = lax.ppermute(grown, axis, [(d, d ^ reach) for d in range(ways)])]
    unnamed x2, blocking collectives: 85.2 us -> 225 us
    all_gather x1 -> x0, waiting for transfers between devices: 87.4 us -> none  [gather_experts(): lax.all_gather(local_pair[0], 'fsdp', axis=1, tiled=True)]
    select_n x0 -> x3, other arithmetic: none -> 21.5 us  [collect(): grown = jnp.where(here & reach == 0, mine_first, theirs_first)]
  transfers between devices with their start and end apart: 12 -> 15, of which waited for: 9 -> 10; matrix products, arithmetic and copies ran while one was open for 31% -> 24% of each run, Pallas kernels for 0% -> 0%
where the time goes in v1:
time: 1430 us; the launch traced here: 1420 us
  waiting for transfers between devices  725 us (51%)
  matrix products  282 us (20%)
  blocking collectives  265 us (19%)
  local copies, waits for them, and re-layouts  66.1 us (5%)
  other arithmetic  43.9 us (3%)
  starting transfers between devices  23.6 us (2%)
  between operations  15.3 us (1%)
    ppermute x4, waiting for transfers between devices, collect(): theirs = lax.ppermute(grown, axis, [(d, d ^ reach) for d in range(ways)])  347 us
    unnamed x2, blocking collectives  225 us
    reduce_scatter x1, waiting for transfers between devices, per_device(): lax.psum_scatter(d_qkv, ('dp', 'fsdp'), scatter_dimension=0, tiled=True)  125 us
    reduce_scatter x1, waiting for transfers between devices, per_device(): lax.psum_scatter(d_proj, ('dp', 'fsdp'), scatter_dimension=0, tiled=True)  102 us
    reduce_scatter x1, waiting for transfers between devices, reduce_experts(): lax.psum_scatter(grad_down.astype(jnp.bfloat16), 'fsdp', scatter_dimensio...  89.5 us
    all_gather x1, blocking collectives, gather_dense(): lax.all_gather(w_router, ('dp', 'fsdp'), axis=0, tiled=True)  40.6 us
    dot_general x1, matrix products, expert_forward(): jnp.einsum('ecd,edf->ecf', expert_rows, w_up, preferred_element_type=jnp....  29.3 us
  transfers between devices with their start and end apart: 15, of which 10 were waited for; matrix products, arithmetic and copies ran while one was open for 24% of the time, Pallas kernels for 0%

profile of v1, /device:TPU:0, one launch (start us, length us, event | category | flops | bytes accessed | tf_op | source)
XLA Modules:
  0.0 1421.8 jit_solution(14740128246822833826)
XLA Ops:
  18.1 60.3 %collective-permute-done.1 = bf16[4,96,3072]{2,1,0:T(8,128)(2,1)} collective-permute-done((bf16[4,96,3072]{2,1,0:T(8,128)(2,1)S(1)}, bf16[4,96,3072]{2,1,0:T(8,128)(2,1)}, u32[]{:S(2)}, u32[]{:S(2)}) %collective-permute-start.1) | collective-permute-done | bytes 2359328 | tf_op jit(solution)/shard_map/ppermute | solution.py:18
  78.5 6.6 maximum_select_fusion.2
  87.3 182.6 %all-reduce.6 = (bf16[768]{0:T(1024)(128)(2,1)S(1)}, bf16[768]{0:T(1024)(128)(2,1)S(1)}) all-reduce(bf16[768]{0:T(1024)(128)(2,1)S(1)} %dynamic-update-slice, bf16[768]{0:T(1024)(128)(2,1)S(1)} %dynamic-update-slice.1), channel_id=1, replica_groups=mesh['dp'=2,'fsdp'=16] {'dp','fsdp'}, use_global_device_ids=true, to_apply=%add | all-reduce | flops 1536 | bytes 6144
  269.9 40.6 %all-gather = bf16[32,24,8]{1,2,0:T(8,128)(2,1)S(1)} all-gather(bf16[1,24,8]{1,2,0:T(8,128)(2,1)S(1)} %bitcast.197), channel_id=1, replica_groups=mesh['dp'=2,'fsdp'=16] {'dp','fsdp'}, dimensions={0}, use_global_device_ids=true | all-gather | bytes 12672 | tf_op jit(solution)/shard_map/all_gather | solution.py:112
  312.5 5.9 convolution_convert_fusion.3
  330.5 12.5 maximum_select_fusion.1
  343.1 37.7 %while.26 = (s32[]{:T(128)}, bf16[12,1,576,64]{2,3,1,0:T(8,128)(2,1)}, f32[12,1,576]{2,1,0:T(1,128)}, bf16[12,1,576,64]{3,2,1,0:T(8,128)(2,1)S(1)}, bf16[12,1,57...) while((s32[]{:T(128)}, bf16[12,1,576,64]{2,3,1,0:T(8,128)(2,1)}, ...), condition=%wide.region_5.6_spmd, body=%wide.region_2.5_spmd.sunk | while | flops 87293376 | bytes 4531033 | solution.py:149
  402.2 18.8 %all-to-all-done.2 = bf16[8,152,768]{2,1,0:T(8,128)(2,1)S(1)} async-done(((bf16[8,152,768]{2,1,0:T(8,128)(2,1)}), bf16[8,152,768]{2,1,0:T(8,128)(2,1)S(1)}, u32[]{:S(2)}, u32[]{:S(2)}) %all-to-all-start.2) | async-done | bytes 1867808 | tf_op jit(solution)/shard_map/all_to_all | solution.py:202
  428.7 20.8 %all-to-all-done = bf16[8,152,768]{2,1,0:T(8,128)(2,1)} async-done(((bf16[8,152,768]{2,1,0:T(8,128)(2,1)}), bf16[8,152,768]{2,1,0:T(8,128)(2,1)}, u32[]{:S(2)}, u32[]{:S(2)}) %all-to-all-start) | async-done | bytes 1867808 | tf_op jit(solution)/shard_map/all_to_all | solution.py:175
  452.4 12.8 fusion.82
  465.2 283.8 %collective-permute-done.3 = bf16[4,384,3072]{2,1,0:T(8,128)(2,1)} collective-permute-done((bf16[4,384,3072]{2,1,0:T(8,128)(2,1)}, bf16[4,384,3072]{2,1,0:T(8,128)(2,1)}, u32[]{:S(2)}, u32[]{:S(2)}) %collective-permute-start.3) | collective-permute-done | bytes 9437216 | tf_op jit(solution)/shard_map/ppermute | solution.py:18
  749.0 29.3 %fusion.43 = (bf16[4,304,3072]{2,1,0:T(8,128)(2,1)}, f32[4,304,3072]{2,1,0:T(8,128)}) fusion(f32[4,304,3072]{2,1,0:T(8,128)} %fusion.82, bf16[4,304,768]{2,1,0:T(8,128)(2,1)} %bitcast.190, bf16[4,384,3072]{2,1,0:T(8,128)(2,1)} %collective-permute-done.3, bf16[4,384,3072]{2,1,0:T(8,128)(2,1)} %maximum_select_fusion.1, pred[]{:T(512)S(6)} %eq.48), kind=kOutput, calls=%fused_computation.60 | convolution fusion | flops 5897453568 | bytes 58097664 | tf_op jit(solution)/shard_map/ecd,edf->ecf/dot_general | solution.py:84
  778.3 16.7 %convolution_convert_fusion.2 = bf16[4,768,3072]{2,1,0:T(8,128)(2,1)} fusion(bf16[4,304,768]{2,1,0:T(8,128)(2,1)} %bitcast.191, bf16[4,304,3072]{2,1,0:T(8,128)(2,1)} %get-tuple-element.212), kind=kOutput, calls=%fused_computation.63 | convolution fusion | flops 5747245056 | bytes 28213248 | tf_op jit(solution)/shard_map/ecd,ecf->edf/dot_general | solution.py:99
  795.2 20.1 %convolution_convert_fusion.1 = bf16[4,3072,768]{2,1,0:T(8,128)(2,1)} fusion(bf16[4,304,768]{2,1,0:T(8,128)(2,1)S(1)} %bitcast.181, f32[4,304,3072]{2,1,0:T(8,128)} %get-tuple-element.213), kind=kOutput, calls=%fused_computation.62 | convolution fusion | flops 5780865024 | bytes 35684352 | tf_op jit(solution)/shard_map/ecf,ecd->efd/dot_general | solution.py:98
  815.4 18.4 %convolution_convert_fusion.6 = bf16[4,304,768]{2,1,0:T(8,128)(2,1)S(1)} fusion(bf16[4,3072,768]{2,1,0:T(8,128)(2,1)} %all-gather.9.cloned.1.call-done, f32[4,304,3072]{2,1,0:T(8,128)} %get-tuple-element.213), kind=kOutput, calls=%fused_computation.91 | convolution fusion | flops 5772361728 | bytes 35684352 | tf_op jit(solution)/shard_map/ecf,efd->ecd/dot_general | solution.py:86
  839.9 18.3 %fusion.57 = bf16[4,304,768]{2,1,0:T(8,128)(2,1)} fusion(bf16[4,304,3072]{2,1,0:T(8,128)(2,1)} %get-tuple-element.212, bf16[4,384,3072]{2,1,0:T(8,128)(2,1)} %collective-permute-done.3, bf16[4,384,3072]{2,1,0:T(8,128)(2,1)} %maximum_select_fusion.1, pred[]{:T(512)S(6)} %eq.48), kind=kOutput, calls=%fused_computation.90 | convolution fusion | flops 5823676416 | bytes 28213248 | tf_op jit(solution)/shard_map/ecf,edf->ecd/dot_general | solution.py:100
  869.9 20.0 %all-to-all-done.3 = bf16[4,304,768]{2,0,1:T(4,128)(2,1)} async-done(((bf16[4,304,768]{2,0,1:T(4,128)(2,1)}), bf16[4,304,768]{2,0,1:T(4,128)(2,1)}, u32[]{:S(2)}, u32[]{:S(2)}) %all-to-all-start.3) | async-done | bytes 1867808 | tf_op jit(solution)/shard_map/all_to_all | solution.py:206
  902.5 6.0 fusion.65
  923.9 100.6 %while.27 = (s32[]{:T(128)}, bf16[12,1,576,64]{2,3,1,0:T(8,128)(2,1)}, bf16[12,1,576,64]{2,3,1,0:T(8,128)(2,1)}, bf16[12,1,576,64]{2,3,1,0:T(8,128)(2,1)}, bf16[...) while((s32[]{:T(128)}, ...), condition=%wide.region_19.20_spmd, body=%wide.region_17.19_spmd.sunk | while | flops 215064000 | bytes 11510129 | solution.py:220
  1035.2 7.2 fusion.63
  1042.5 42.1 %all-reduce.5 = (f32[768]{0:T(1024)S(1)}, f32[768]{0:T(1024)S(1)}, f32[768,8]{0,1:T(8,128)S(1)}) all-reduce(f32[768]{0:T(1024)S(1)} %get-tuple-element.158, f32[768]{0:T(1024)S(1)} %get-tuple-element.156, f32[768,8]{0,1:T(8,128)S(1)} %fusion.84), channel_id=2, replica_groups=mesh['dp'=2,'fsdp'=16] {'dp','fsdp'}, use_global_device_ids=true, to_apply=%region_23.24.clone | all-reduce | flops 7680 | bytes 61440
  1095.7 89.5 %reduce-scatter.12.cloned.1.call-done = bf16[4,192,768]{2,1,0:T(8,128)(2,1)} async-done(((bf16[4,3072,768]{2,1,0:T(8,128)(2,1)}), bf16[4,192,768]{2,1,0:T(8,128)(2,1)}) %reduce-scatter.12.cloned.1.call-update) | async-done | bytes 1179664 | tf_op jit(solution)/shard_map/reduce_scatter | solution.py:129
  1188.0 101.6 %reduce-scatter.8.cloned.1.call-done = f32[24,768]{1,0:T(8,128)} async-done(((f32[768,768]{1,0:T(8,128)}), f32[24,768]{1,0:T(8,128)}) %reduce-scatter.8.cloned.1.call-update) | async-done | bytes 73744 | tf_op jit(solution)/shard_map/reduce_scatter | solution.py:238
  1289.6 124.9 %reduce-scatter.6.cloned.1.call-done = f32[24,2304]{1,0:T(8,128)} async-done(((f32[768,2304]{1,0:T(8,128)}), f32[24,2304]{1,0:T(8,128)}) %reduce-scatter.6.cloned.1.call-update) | async-done | bytes 221200 | tf_op jit(solution)/shard_map/reduce_scatter | solution.py:237
  (356 shorter events, 267.3 us)
Async XLA Ops:
  7.2 305.3 %all-gather.5.cloned.1.call-start = ((), (), s32[]{:S(2)}) async-start(), calls=%async_computation.8 | async-start | bytes 3649536 | tf_op jit(solution)/shard_map/all_gather | solution.py:109
  7.9 372.9 %all-gather.7.cloned.1.call-start = ((), (), s32[]{:S(2)}) async-start(), calls=%async_computation.9 | async-start | bytes 1216512 | tf_op jit(solution)/shard_map/all_gather | solution.py:110
  8.7 443.7 %all-gather.9.cloned.1.call-start = ((), (), s32[]{:S(2)}) async-start(), calls=%async_computation.10 | async-start | bytes 20054016 | tf_op jit(solution)/shard_map/all_gather | solution.py:120
  9.4 3.4 collective-permute-start
  15.2 63.3 %collective-permute-start.1 = (bf16[4,96,3072]{2,1,0:T(8,128)(2,1)S(1)}, bf16[4,96,3072]{2,1,0:T(8,128)(2,1)}, u32[]{:S(2)}, u32[]{:S(2)}) collective-permute-start(bf16[4,96,3072]{2,1,0:T(8,128)(2,1)S(1)} %maximum_select_fusion.5), channel_id=1, source_target_pairs={{0,2},{1,3},{2,0},{3,1},{4,6},{5,7},{6,4},{7,5},{8,10},{9,11},{10,... | collective-permute-start | bytes 7077896 | tf_op jit(solution)/shard_map/ppermute | solution.py:18
  18.1 68.8 %copy-start.52 = (bf16[24]{0:T(256)(128)(2,1)S(1)}, bf16[24]{0:T(256)(128)(2,1)}, u32[]{:S(2)}) copy-start(bf16[24]{0:T(256)(128)(2,1)} %param.16) | copy-start | bytes 148
  18.1 69.0 %copy-start.53 = (bf16[24]{0:T(256)(128)(2,1)S(1)}, bf16[24]{0:T(256)(128)(2,1)}, u32[]{:S(2)}) copy-start(bf16[24]{0:T(256)(128)(2,1)} %param.19) | copy-start | bytes 148
  18.1 251.8 %copy-start.50 = (bf16[24,8]{0,1:T(8,128)(2,1)S(1)}, bf16[24,8]{0,1:T(8,128)(2,1)}, u32[]{:S(2)}) copy-start(bf16[24,8]{0,1:T(8,128)(2,1)} %param.20) | copy-start | bytes 1156
  18.1 292.5 %copy-start.8 = (bf16[576,768]{1,0:T(8,128)(2,1)S(1)}, bf16[576,768]{1,0:T(8,128)(2,1)}, u32[]{:S(2)}) copy-start(bf16[576,768]{1,0:T(8,128)(2,1)} %param.15) | copy-start | bytes 2654212
  85.1 226.2 %copy-start.36 = (s32[576,2]{0,1:T(2,128)S(1)}, s32[576,2]{0,1:T(2,128)}, u32[]{:S(2)}) copy-start(s32[576,2]{0,1:T(2,128)} %param.24) | copy-start | bytes 13828
  85.1 226.8 %copy-start.38 = (s32[576,2]{0,1:T(2,128)S(1)}, s32[576,2]{0,1:T(2,128)}, u32[]{:S(2)}) copy-start(s32[576,2]{0,1:T(2,128)} %param.23) | copy-start | bytes 13828
  85.1 245.5 %collective-permute-start.2 = (bf16[4,192,3072]{2,1,0:T(8,128)(2,1)}, bf16[4,192,3072]{2,1,0:T(8,128)(2,1)}, u32[]{:S(2)}, u32[]{:S(2)}) collective-permute-start(bf16[4,192,3072]{2,1,0:T(8,128)(2,1)} %maximum_select_fusion.2), channel_id=1, source_target_pairs={{0,4},{1,5},{2,6},{3,7},{4,0},{5,1},{6,2},{7,3},{8,12},{9,13},{10,... | collective-permute-start | bytes 14155784 | tf_op jit(solution)/shard_map/ppermute | solution.py:18
  269.9 115.4 %copy-start.32 = (f32[768]{0:T(1024)}, f32[768]{0:T(1024)S(1)}, u32[]{:S(2)}) copy-start(f32[768]{0:T(1024)S(1)} %convert_element_type.104) | copy-start | bytes 9220
  310.6 75.3 %copy-start.24 = (bf16[768,8]{0,1:T(8,128)(2,1)}, bf16[768,8]{0,1:T(8,128)(2,1)S(1)}, u32[]{:S(2)}) copy-start(bf16[768,8]{0,1:T(8,128)(2,1)S(1)} %reshape.231) | copy-start | bytes 36868
  343.1 405.9 %collective-permute-start.3 = (bf16[4,384,3072]{2,1,0:T(8,128)(2,1)}, bf16[4,384,3072]{2,1,0:T(8,128)(2,1)}, u32[]{:S(2)}, u32[]{:S(2)}) collective-permute-start(bf16[4,384,3072]{2,1,0:T(8,128)(2,1)} %maximum_select_fusion.1), channel_id=1, source_target_pairs={{0,8},{1,9},{2,10},{3,11},{4,12},{5,13},{6,14},{7,15},{8,0},{9,1},... | collective-permute-start | bytes 28311560 | tf_op jit(solution)/shard_map/ppermute | solution.py:18
  393.8 27.2 %all-to-all-start.2 = ((bf16[8,152,768]{2,1,0:T(8,128)(2,1)}), bf16[8,152,768]{2,1,0:T(8,128)(2,1)S(1)}, u32[]{:S(2)}, u32[]{:S(2)}) async-start(bf16[8,152,768]{2,1,0:T(8,128)(2,1)} %bitcast.192), calls=%async_computation.2 | async-start | bytes 3735552 | tf_op jit(solution)/shard_map/all_to_all | solution.py:202
  422.3 27.2 %all-to-all-start = ((bf16[8,152,768]{2,1,0:T(8,128)(2,1)}), bf16[8,152,768]{2,1,0:T(8,128)(2,1)}, u32[]{:S(2)}, u32[]{:S(2)}) async-start(bf16[8,152,768]{2,1,0:T(8,128)(2,1)} %bitcast.189), calls=%async_computation | async-start | bytes 3735552 | tf_op jit(solution)/shard_map/all_to_all | solution.py:175
  427.0 665.7 %reduce-scatter.10.cloned.1.call-start = ((), (), s32[]{:S(2)}) async-start(), calls=%async_computation.13 | async-start | bytes 20054016 | tf_op jit(solution)/shard_map/reduce_scatter | solution.py:126
  795.0 390.1 %reduce-scatter.12.cloned.1.call-start = ((), (), s32[]{:S(2)}) async-start(), calls=%async_computation.14 | async-start | bytes 20054016 | tf_op jit(solution)/shard_map/reduce_scatter | solution.py:129
  836.0 26.8 %all-to-all-start.1 = ((bf16[4,304,768]{2,0,1:T(4,128)(2,1)}), bf16[4,304,768]{2,0,1:T(4,128)(2,1)S(1)}, u32[]{:S(2)}, u32[]{:S(2)}) async-start(bf16[4,304,768]{2,0,1:T(4,128)(2,1)} %copy.108), calls=%async_computation.1 | async-start | bytes 3735552 | tf_op jit(solution)/shard_map/all_to_all | solution.py:177
  862.8 27.0 %all-to-all-start.3 = ((bf16[4,304,768]{2,0,1:T(4,128)(2,1)}), bf16[4,304,768]{2,0,1:T(4,128)(2,1)}, u32[]{:S(2)}, u32[]{:S(2)}) async-start(bf16[4,304,768]{2,0,1:T(4,128)(2,1)} %copy.112), calls=%async_computation.3 | async-start | bytes 3735552 | tf_op jit(solution)/shard_map/all_to_all | solution.py:206
  867.6 422.0 %reduce-scatter.8.cloned.1.call-start = ((), (), s32[]{:S(2)}) async-start(), calls=%async_computation.12 | async-start | bytes 2433024 | tf_op jit(solution)/shard_map/reduce_scatter | solution.py:238
  923.6 490.9 %reduce-scatter.6.cloned.1.call-start = ((), (), s32[]{:S(2)}) async-start(), calls=%async_computation.11 | async-start | bytes 7299072 | tf_op jit(solution)/shard_map/reduce_scatter | solution.py:237
  1035.2 51.2 %copy-start.10 = (bf16[576,768]{1,0:T(8,128)(2,1)S(1)}, bf16[576,768]{1,0:T(8,128)(2,1)}, u32[]{:S(2)}) copy-start(bf16[576,768]{1,0:T(8,128)(2,1)} %param.15) | copy-start | bytes 2654212
  (45 other events, 213.8 us)
Sparse Core Ops, SparseCore 0:
  10.9 68.8 all-gather.4
  82.7 53.3 all-gather.6
  137.7 147.9 all-gather.8
  795.1 191.7 reduce-scatter.9
  990.9 194.2 reduce-scatter.11
  1190.8 98.6 reduce-scatter.7
  1295.8 118.6 reduce-scatter.5
